TPU v7x, 32 devices: a whole 2x2x4 slice. The times are simulated.
32 devices in a mesh: dp: 4 (over z), mp: 8 (over y, x, core).
Axes of the slice: x: 2, y: 2, z: 4, core: 2. Of those that a mesh axis runs over, the one named last changes fastest.
Arguments:
- features: bfloat16 [256, 256, 1, 16, 64], P('mp', None, None, 'dp'), may hold values from -6 to 6
- out_grad: bfloat16 [256, 256, 1, 16, 64], P('mp', None, None, 'dp'), may hold values from -6 to 6
- spectral_weight: bfloat16 [16, 32, 32, 64, 128], P('dp', 'mp'), may hold values from -1.5 to 1.5
- local_weight: bfloat16 [64, 64], replicated, may hold values from -0.75 to 0.75
Outputs:
- layer_out: bfloat16 [256, 256, 1, 16, 64], P('mp', None, None, 'dp')
- feature_grad: bfloat16 [256, 256, 1, 16, 64], P('mp', None, None, 'dp')
- spectral_grad: float32 [16, 32, 32, 64, 128], P('dp', 'mp')
- local_grad: float32 [64, 64], replicated
All inputs are finite; a program needn't handle non-finite values.
Results may differ from a plain program's by a relative error of at most 0.03.
Values may be sent and summed in bfloat16 or wider, within the bound.
No kernel may reach another device: no remote copies, remote signals or barrier semaphores. Data moves between devices by JAX's collectives and lax.ppermute only.
A program may use at most 192 MiB of HBM per device.

v0:
```python
import math
import jax
import jax.numpy as jnp
from jax import lax
from jax.sharding import PartitionSpec as P

NX = 256
NY = 256
KX = 32
KY = 32
SNAP = 1


def make_tables(slab_count):
    y_index = jnp.arange(NY, dtype=jnp.int32)
    k_index = jnp.arange(KY, dtype=jnp.int32)
    y_angle = 2.0 * math.pi / NY * (k_index[:, None] * y_index[None, :] % NY).astype(jnp.float32)
    y_scale = 1.0 / math.sqrt(NY)
    y_table = jnp.stack([jnp.cos(y_angle) * y_scale, -jnp.sin(y_angle) * y_scale]).astype(
        jnp.bfloat16
    )
    k_weight = jnp.where(k_index == 0, 1.0, 2.0).astype(jnp.float32)
    y_back = (jnp.transpose(y_table.astype(jnp.float32), (2, 0, 1)) * k_weight).astype(jnp.bfloat16)
    stored_index = jnp.arange(NX, dtype=jnp.int32)
    slab_rows = NX // slab_count
    x_index = stored_index % slab_rows * slab_count + stored_index // slab_rows
    frequency = jnp.arange(KX, dtype=jnp.int32) - KX // 2
    x_angle = 2.0 * math.pi / NX * (frequency[:, None] * x_index[None, :] % NX).astype(jnp.float32)
    x_scale = 1.0 / math.sqrt(NX)
    x_cosine = jnp.cos(x_angle) * x_scale
    x_sine = jnp.sin(x_angle) * x_scale
    x_table = jnp.stack(
        [jnp.stack([x_cosine, x_sine], 1), jnp.stack([-x_sine, x_cosine], 1)]
    ).astype(jnp.bfloat16)
    x_back = jnp.transpose(x_table, (2, 3, 0, 1))
    return (y_table, y_back, x_table, x_back)


def product(form, left, right):
    return jnp.einsum(form, left, right, preferred_element_type=jnp.float32)


def block_weights(weights):
    channels = weights.shape[-1] // 2
    w_real = weights[..., :channels]
    w_imag = weights[..., channels:]
    upper = jnp.concatenate([w_real, w_imag], -1)
    lower = jnp.concatenate([-w_imag, w_real], -1)
    return jnp.concatenate([upper, lower], -2)


def to_items(coeffs, snaps, zcount):
    mode_rows, _, kx_count, columns = coeffs.shape
    channels = columns // (snaps * zcount)
    shaped = coeffs.reshape(mode_rows, 2, kx_count, snaps, zcount, channels).transpose(
        4, 0, 2, 3, 1, 5
    )
    return shaped.reshape(zcount, mode_rows * kx_count, snaps, 2 * channels)


def from_items(mode_items, mode_rows, snaps):
    zcount, total, _, double = mode_items.shape
    channels = double // 2
    kx_count = total // mode_rows
    shaped = mode_items.reshape(zcount, mode_rows, kx_count, snaps, 2, channels).transpose(
        1, 4, 2, 3, 0, 5
    )
    return shaped.reshape(mode_rows, 2, kx_count, snaps * zcount * channels)


def combine(gram_blocks, mode_rows):
    channels = gram_blocks.shape[-1] // 2
    top_left = gram_blocks[..., :channels, :channels]
    top_right = gram_blocks[..., :channels, channels:]
    low_left = gram_blocks[..., channels:, :channels]
    low_right = gram_blocks[..., channels:, channels:]
    joined = jnp.concatenate([top_left + low_right, top_right - low_left], -1)
    return joined.reshape(gram_blocks.shape[0], mode_rows, -1, channels, 2 * channels)


def activation(values):
    return jax.nn.gelu(values, approximate=True)


def body(features, out_grad, spectral_weight, local_weight):
    y_table, y_back, x_table, x_back = make_tables(lax.axis_size("mp"))
    rows_here, grid_y, snaps, zcount, channels = features.shape
    columns = snaps * zcount * channels
    mode_rows = spectral_weight.shape[1]
    offset = lax.axis_index("mp") * rows_here
    x_back_own = lax.dynamic_slice_in_dim(x_back, offset, rows_here, 1)
    x_table_own = lax.dynamic_slice_in_dim(x_table, offset, rows_here, 3)

    def to_modes(spectrum):
        return lax.psum_scatter(
            product("ojrx,xrkq->kojq", x_table_own, spectrum).astype(jnp.bfloat16),
            "mp",
            scatter_dimension=0,
            tiled=True,
        )

    def to_rows(coeffs):
        return product(
            "rxoj,kojq->xrkq", x_back_own, lax.all_gather(coeffs, "mp", axis=0, tiled=True)
        ).astype(jnp.bfloat16)

    flat_field = features.reshape(rows_here, grid_y, columns)
    spectrum_y = product("xyq,rky->xrkq", flat_field, y_table).astype(jnp.bfloat16)
    mode_coeffs = to_modes(spectrum_y)
    blocks = block_weights(spectral_weight).reshape(zcount, -1, 2 * channels, 2 * channels)
    mode_items = to_items(mode_coeffs, snaps, zcount)
    mixed_items = product("zmpi,zmio->zmpo", mode_items, blocks).astype(jnp.bfloat16)
    grid_rows = to_rows(from_items(mixed_items, mode_rows, snaps))
    local_part = jnp.dot(
        features.reshape(-1, channels), local_weight, preferred_element_type=jnp.float32
    )
    preact = product("yrk,xrkq->xyq", y_back, grid_rows) + local_part.reshape(
        rows_here, grid_y, columns
    )
    output, pullback = jax.vjp(activation, preact)
    preact_grad = pullback(out_grad.reshape(rows_here, grid_y, columns).astype(jnp.float32))[
        0
    ].astype(jnp.bfloat16)
    local_term = jnp.dot(
        features.reshape(-1, channels).T,
        preact_grad.reshape(-1, channels),
        preferred_element_type=jnp.float32,
    )
    grad_scale = 1.0 / math.sqrt(NX * NY * SNAP * lax.axis_size("dp") * zcount)
    local_grad = lax.psum(local_term, ("dp", "mp")) * grad_scale
    rows_grad = product("yrk,xyq->xrkq", y_back, preact_grad).astype(jnp.bfloat16)
    mixed_grad = to_modes(rows_grad)
    grad_items = to_items(mixed_grad, snaps, zcount)
    gram_blocks = product("zmpi,zmpo->zmio", mode_items, grad_items)
    spectral_grad = combine(gram_blocks, mode_rows)
    back_items = product("zmpo,zmio->zmpi", grad_items, blocks).astype(jnp.bfloat16)
    spectrum_grad = to_rows(from_items(back_items, mode_rows, snaps))
    local_back = jnp.dot(
        preact_grad.reshape(-1, channels), local_weight.T, preferred_element_type=jnp.float32
    )
    back_field = product("rky,xrkq->xyq", y_table, spectrum_grad) + local_back.reshape(
        rows_here, grid_y, columns
    )
    layer_out = output.astype(jnp.bfloat16).reshape(features.shape)
    feature_grad = back_field.astype(jnp.bfloat16).reshape(features.shape)
    return (layer_out, feature_grad, spectral_grad, local_grad)


def solution(mesh):
    placed = (
        P("mp", None, None, "dp", None),
        P("mp", None, None, "dp", None),
        P("dp", "mp", None, None, None),
        P(),
    )
    return jax.shard_map(
        body,
        mesh=mesh,
        in_specs=placed,
        out_specs=(
            P("mp", None, None, "dp", None),
            P("mp", None, None, "dp", None),
            P("dp", "mp", None, None, None),
            P(),
        ),
        check_vma=False,
    )
```

profile of v0, /device:TPU:0, one launch (start us, length us, event | category | flops | bytes accessed | tf_op | source)
XLA Modules:
  0.0 325.2 jit_solution(8694081158683600945)
XLA Ops:
  7.7 3.6 %fusion.16 = bf16[32,2,32,256,1]{3,2,0,1,4:T(8,128)(2,1)S(1)} fusion(bf16[32,256,256,1]{1,2,0,3:T(8,128)(2,1)} %bitcast.172, bf16[1,32,256]{2,1,0:T(8,128)(2,1)S(1)} %get-tuple-element.31, bf16[1,32,256]{2,1,0:T(8,128)(2,1)S(1)} %get-tuple-element.32), kind=kOutput, calls=%fused_computation.32 | convolution fusion | flops 269025280 | bytes 5275648 | tf_op jit(solution)/shard_map/xyq,rky->xrkq/dot_general | solution.py:40
  11.3 1.9 fusion.20
  13.2 9.1 %slice_negate_fusion = (bf16[4,4,32,64,64]{4,3,2,1,0:T(8,128)(2,1)S(1)}, bf16[4,4,32,64,64]{4,3,2,1,0:T(8,128)(2,1)S(1)}) fusion(bf16[4,4,32,64,128]{4,3,2,1,0:T(8,128)(2,1)} %param.6), kind=kLoop, calls=%fused_computation.23 | loop fusion | flops 2097152 | bytes 16777216 | tf_op jit(solution)/shard_map/neg | solution.py:48
  22.3 14.4 %maximum_maximum_fusion = bf16[4,4,32,128,128]{4,3,2,1,0:T(8,128)(2,1)} fusion(bf16[4,4,32,64,64]{4,3,2,1,0:T(8,128)(2,1)S(1)} %get-tuple-element.25, bf16[4,4,32,64,64]{4,3,2,1,0:T(8,128)(2,1)S(1)} %get-tuple-element.24, bf16[4,4,32,64,128]{4,3,2,1,0:T(8,128)(2,1)} %param.6), kind=kLoop, calls=%fused_computation.2 | loop fusion | flops 50331648 | bytes 33554432 | tf_op jit(solution)/shard_map/concatenate | solution.py:49
  36.7 15.4 %reduce-scatter.3.cloned.1.call-done = bf16[4,2,32,256]{3,2,1,0:T(8,128)(2,1)} async-done(((bf16[32,2,32,256]{3,2,1,0:T(8,128)(2,1)}), bf16[4,2,32,256]{3,2,1,0:T(8,128)(2,1)}) %reduce-scatter.3.cloned.1.call-update) | async-done | bytes 131088 | tf_op jit(solution)/shard_map/reduce_scatter | solution.py:95
  53.6 8.0 %fusion.55 = f32[4,128,1,128]{3,2,1,0:T(1,128)S(1)} fusion(bf16[4,128,128,1]{2,3,1,0:T(2,128)(2,1)S(1)} %reshape.391, bf16[4,128,128,128]{3,2,1,0:T(8,128)(2,1)} %bitcast.167), kind=kOutput, calls=%fused_computation.97 | convolution fusion | flops 16777216 | bytes 17170432 | tf_op jit(solution)/shard_map/zmpi,zmio->zmpo/dot_general | solution.py:40
  63.1 12.6 %copy.49 = bf16[32,256,1,4,64]{4,3,1,0,2:T(4,128)(2,1)} copy(bf16[32,256,1,4,64]{1,4,3,2,0:T(8,128)(2,1)} %param.4) | data formatting | bytes 8388608 | tf_op args[0]
  75.8 11.9 %fusion.56 = f32[32768,64]{1,0:T(8,128)} fusion(bf16[32768,64]{1,0:T(8,128)(2,1)} %bitcast.169, bf16[64,64]{1,0:T(8,128)(2,1)S(1)} %copy-done), kind=kOutput, calls=%fused_computation.98 | convolution fusion | flops 268435456 | bytes 12591104 | tf_op jit(solution)/shard_map/dot_general | solution.py:114
  87.6 14.3 %reshape.358 = f32[32,256,256]{2,1,0:T(8,128)} reshape(f32[32768,64]{1,0:T(8,128)} %fusion.56) | data formatting | bytes 16777216 | tf_op jit(solution)/shard_map/reshape | solution.py:117
  102.0 8.9 %copy.51 = f32[32,256,256]{1,2,0:T(8,128)} copy(f32[32,256,256]{2,1,0:T(8,128)} %reshape.358) | data formatting | bytes 16777216 | tf_op jit(solution)/shard_map/reshape | solution.py:117
  112.8 12.0 %fusion.2 = (bf16[32,256,256]{1,2,0:T(8,128)(2,1)S(1)}, bf16[32,256,256]{1,2,0:T(8,128)(2,1)}) fusion(bf16[32,256,1,4,64]{1,4,3,2,0:T(8,128)(2,1)} %param.5, f32[32,256,256]{1,2,0:T(8,128)} %copy.51, f32[32]{0:T(128)S(1)} %compare_select_fusion, bf16[1,32,256]{2,1,0:T(8,128)(2,1)S(1)} %get-tuple-element.31, bf16[1,32,256]{2,1,0:T(8,128)(2,1)S(1)} %get-tuple-element.32, ...), kind=kOutput, calls=%fused_computation.11 | convolution fusion | flops 318832640 | bytes 22052992 | tf_op jit(solution)/shard_map/yrk,xrkq->xyq/dot_general | solution.py:40
  124.8 2.0 copy-done.2
  128.2 6.4 %copy.58 = bf16[32,256,256]{2,1,0:T(8,128)(2,1)} copy(bf16[32,256,256]{1,2,0:T(8,128)(2,1)} %copy-done.2) | data formatting | bytes 8388608 | tf_op jit(solution)/shard_map/convert_element_type | solution.py:123
  136.6 11.2 %reshape.364 = bf16[32768,64]{1,0:T(8,128)(2,1)} reshape(bf16[32,256,256]{2,1,0:T(8,128)(2,1)} %copy.58) | data formatting | bytes 8388608 | tf_op jit(solution)/shard_map/reshape | solution.py:139
  147.7 8.2 %convolution_bitcast_fusion = f32[64,64]{0,1:T(8,128)S(1)} fusion(bf16[32768,64]{1,0:T(8,128)(2,1)} %reshape.364, bf16[32768,64]{1,0:T(8,128)(2,1)} %bitcast.170), kind=kOutput, calls=%fused_computation.38 | convolution fusion | flops 268435456 | bytes 8404992 | tf_op jit(solution)/shard_map/dot_general | solution.py:124
  155.9 39.8 %psum.7 = f32[64,64]{0,1:T(8,128)S(1)} all-reduce(f32[64,64]{0,1:T(8,128)S(1)} %convolution_bitcast_fusion), channel_id=1, replica_groups=mesh['dp'=4,'mp'=8] {'dp','mp'}, use_global_device_ids=true, to_apply=%region_2.3 | all-reduce | flops 4096 | bytes 32768 | tf_op jit(solution)/shard_map/psum | solution.py:130
  196.4 11.9 %fusion.58 = f32[32768,64]{1,0:T(8,128)} fusion(bf16[32768,64]{1,0:T(8,128)(2,1)} %reshape.364, bf16[64,64]{1,0:T(8,128)(2,1)S(1)} %copy-done), kind=kOutput, calls=%fused_computation.100 | convolution fusion | flops 268435456 | bytes 12591104 | tf_op jit(solution)/shard_map/dot_general | solution.py:138
  208.2 14.4 %reshape.365 = f32[32,256,256]{2,1,0:T(8,128)} reshape(f32[32768,64]{1,0:T(8,128)} %fusion.58) | data formatting | bytes 16777216 | tf_op jit(solution)/shard_map/reshape | solution.py:141
  222.6 9.0 %copy.60 = f32[32,256,256]{1,2,0:T(8,128)} copy(f32[32,256,256]{2,1,0:T(8,128)} %reshape.365) | data formatting | bytes 16777216 | tf_op jit(solution)/shard_map/reshape | solution.py:141
  233.3 12.2 %fusion.57 = f32[4,128,1,128]{3,2,1,0:T(1,128)S(1)} fusion(bf16[4,128,128,1]{2,3,1,0:T(2,128)(2,1)S(1)} %reshape.393, bf16[4,128,128,128]{3,2,1,0:T(8,128)(2,1)} %bitcast.168), kind=kOutput, calls=%fused_computation.99 | convolution fusion | flops 16777216 | bytes 17170432 | tf_op jit(solution)/shard_map/zmpo,zmio->zmpi/dot_general | solution.py:40
  246.8 11.4 %broadcast_multiply_fusion = f32[4,128,128,128]{3,2,1,0:T(8,128)} fusion(f32[4,128,128]{2,1,0:T(8,128)S(1)} %convert.35, f32[4,128,128]{2,1,0:T(8,128)S(1)} %convert.34), kind=kLoop, calls=%fused_computation.4 | loop fusion | flops 8388608 | bytes 34078720 | tf_op jit(solution)/shard_map/zmpi,zmpo->zmio/dot_general | solution.py:40
  258.3 34.2 %slice_add_fusion = (f32[4,128,64,64]{3,2,1,0:T(8,128)}, f32[4,128,64,64]{3,2,1,0:T(8,128)}) fusion(f32[4,128,128,128]{3,2,1,0:T(8,128)} %broadcast_multiply_fusion), kind=kLoop, calls=%fused_computation.1 | loop fusion | flops 4194304 | bytes 50331648 | tf_op jit(solution)/shard_map/add | solution.py:77
  292.5 17.0 %pad_maximum_fusion = f32[4,128,64,128]{3,2,1,0:T(8,128)} fusion(f32[4,128,64,64]{3,2,1,0:T(8,128)} %get-tuple-element.21, f32[4,128,64,64]{3,2,1,0:T(8,128)} %get-tuple-element.20), kind=kLoop, calls=%fused_computation.3 | loop fusion | flops 4194304 | bytes 33554432 | tf_op jit(solution)/shard_map/concatenate | solution.py:77
  311.2 7.5 %fusion.10 = bf16[32,256,256]{1,2,0:T(8,128)(2,1)} fusion(f32[32,256,256]{1,2,0:T(8,128)} %copy.60, bf16[32,2,32,256]{3,0,1,2:T(8,128)(2,1)S(1)} %fusion.23, bf16[1,32,256]{2,1,0:T(8,128)(2,1)S(1)} %get-tuple-element.31, bf16[1,32,256]{2,1,0:T(8,128)(2,1)S(1)} %get-tuple-element.32), kind=kOutput, calls=%fused_computation.20 | convolution fusion | flops 272646144 | bytes 13664256 | tf_op jit(solution)/shard_map/rky,xrkq->xyq/dot_general | solution.py:40
  (47 shorter events, 14.1 us)
Async XLA Ops:
  7.2 68.6 %copy-start = (bf16[64,64]{1,0:T(8,128)(2,1)S(1)}, bf16[64,64]{1,0:T(8,128)(2,1)}, u32[]{:S(2)}) copy-start(bf16[64,64]{1,0:T(8,128)(2,1)} %param.7) | copy-start | bytes 24580
  7.2 44.9 %reduce-scatter.3.cloned.1.call-start = ((), (), s32[]{:S(2)}) async-start(), calls=%async_computation.2 | async-start | bytes 1179648 | tf_op jit(solution)/shard_map/reduce_scatter | solution.py:95
  13.2 97.9 %all-gather.3.cloned.1.call-start = ((), (), s32[]{:S(2)}) async-start(), calls=%async_computation.3 | async-start | bytes 1179648 | tf_op jit(solution)/shard_map/all_gather | solution.py:104
  62.9 168.7 %reduce-scatter.5.cloned.1.call-start = ((), (), s32[]{:S(2)}) async-start(), calls=%async_computation.4 | async-start | bytes 1179648 | tf_op jit(solution)/shard_map/reduce_scatter | solution.py:95
  124.8 2.0 copy-start.2
  136.5 173.0 %all-gather.5.cloned.1.call-start = ((), (), s32[]{:S(2)}) async-start(), calls=%async_computation.5 | async-start | bytes 1179648 | tf_op jit(solution)/shard_map/all_gather | solution.py:104
  292.5 26.2 %copy-start.1 = (bf16[64,64]{1,0:T(8,128)(2,1)S(1)}, bf16[64,64]{1,0:T(8,128)(2,1)}, u32[]{:S(2)}) copy-start(bf16[64,64]{1,0:T(8,128)(2,1)} %param.7) | copy-start | bytes 24580
Sparse Core Ops, SparseCore 0:
  13.3 38.7 reduce-scatter.2
  63.0 23.4 all-gather.2
  136.6 36.3 reduce-scatter.4
  246.9 24.1 all-gather.4
where the time goes:
time: 328 us; the launch traced here: 325 us
  other arithmetic  86.7 us (26%)
  local copies, waits for them, and re-layouts  85.2 us (26%)
  matrix products  83.7 us (26%)
  blocking collectives  39.8 us (12%)
  waiting for transfers between devices  15.5 us (5%)
  between operations  14 us (4%)
    dot_general x10, matrix products, product(): return jnp.einsum(form, left, right, preferred_element_type=jnp.float32)  51.8 us
    psum x1, blocking collectives, body(): local_grad = lax.psum(local_term, ('dp', 'mp')) * grad_scale  39.8 us
    add x1, other arithmetic, combine(): joined = jnp.concatenate([top_left + low_right, top_right - low_left], -1)  34.2 us
    reshape x2, local copies, waits for them, and re-layouts, body(): local_back.reshape(rows_here, grid_y, columns)  23.4 us
    reshape x2, local copies, waits for them, and re-layouts, body(): local_part.reshape(rows_here, grid_y, columns)  23.3 us
    concatenate x1, other arithmetic, combine(): joined = jnp.concatenate([top_left + low_right, top_right - low_left], -1)  17 us
    reduce_scatter x2, waiting for transfers between devices, to_modes(): lax.psum_scatter(product('ojrx,xrkq->kojq', x_table_own, spectrum).astype...  15.4 us
    unnamed x8, local copies, waits for them, and re-layouts  15.3 us
  transfers between devices with their start and end apart: 4, of which 1 were waited for; matrix products, arithmetic and copies ran while one was open for 58% of the time, Pallas kernels for 0%

commit v1 on v0

--- a/solution.py
+++ b/solution.py
@@ -3,6 +3,7 @@
 import jax.numpy as jnp
 from jax import lax
 from jax.sharding import PartitionSpec as P
+from jax.lax import psum
 
 NX = 256
 NY = 256
@@ -127,7 +128,12 @@
         preferred_element_type=jnp.float32,
     )
     grad_scale = 1.0 / math.sqrt(NX * NY * SNAP * lax.axis_size("dp") * zcount)
-    local_grad = lax.psum(local_term, ("dp", "mp")) * grad_scale
+
+    def _attach_record(inner_x):
+        p_next = psum(psum(inner_x, axis_name="dp"), axis_name="mp")
+        return p_next
+
+    local_grad = _attach_record(local_term) * grad_scale
     rows_grad = product("yrk,xyq->xrkq", y_back, preact_grad).astype(jnp.bfloat16)
     mixed_grad = to_modes(rows_grad)
     grad_items = to_items(mixed_grad, snaps, zcount)

time: 328 us -> 330 us (level)
    psum x1 -> x2, blocking collectives: 39.8 us -> 41.7 us  [_attach_record(): p_next = psum(psum(inner_x, axis_name='dp'), axis_name='mp')]
where the time goes in v1:
time: 330 us; the launch traced here: 327 us
  other arithmetic  86.8 us (26%)
  local copies, waits for them, and re-layouts  85.2 us (26%)
  matrix products  83.6 us (25%)
  blocking collectives  41.7 us (13%)
  waiting for transfers between devices  15.5 us (5%)
  between operations  14 us (4%)
    dot_general x10, matrix products, product(): return jnp.einsum(form, left, right, preferred_element_type=jnp.float32)  51.7 us
    psum x2, blocking collectives, _attach_record(): p_next = psum(psum(inner_x, axis_name='dp'), axis_name='mp')  41.7 us
    add x1, other arithmetic, combine(): joined = jnp.concatenate([top_left + low_right, top_right - low_left], -1)  34.3 us
    reshape x2, local copies, waits for them, and re-layouts, body(): local_back.reshape(rows_here, grid_y, columns)  23.4 us
    reshape x2, local copies, waits for them, and re-layouts, body(): local_part.reshape(rows_here, grid_y, columns)  23.3 us
    concatenate x1, other arithmetic, combine(): joined = jnp.concatenate([top_left + low_right, top_right - low_left], -1)  17 us
    reduce_scatter x2, waiting for transfers between devices, to_modes(): lax.psum_scatter(product('ojrx,xrkq->kojq', x_table_own, spectrum).astype...  15.4 us
    unnamed x8, local copies, waits for them, and re-layouts  15.3 us
  transfers between devices with their start and end apart: 4, of which 1 were waited for; matrix products, arithmetic and copies ran while one was open for 58% of the time, Pallas kernels for 0%

profile of v1, /device:TPU:0, one launch (start us, length us, event | category | flops | bytes accessed | tf_op | source)
XLA Modules:
  0.0 327.1 jit_solution(12823412788867126916)
XLA Ops:
  7.7 3.6 %fusion.16 = bf16[32,2,32,256,1]{3,2,0,1,4:T(8,128)(2,1)S(1)} fusion(bf16[32,256,256,1]{1,2,0,3:T(8,128)(2,1)} %bitcast.172, bf16[1,32,256]{2,1,0:T(8,128)(2,1)S(1)} %get-tuple-element.31, bf16[1,32,256]{2,1,0:T(8,128)(2,1)S(1)} %get-tuple-element.32), kind=kOutput, calls=%fused_computation.32 | convolution fusion | flops 269025280 | bytes 5275648 | tf_op jit(solution)/shard_map/xyq,rky->xrkq/dot_general | solution.py:41
  13.2 9.1 %slice_negate_fusion = (bf16[4,4,32,64,64]{4,3,2,1,0:T(8,128)(2,1)S(1)}, bf16[4,4,32,64,64]{4,3,2,1,0:T(8,128)(2,1)S(1)}) fusion(bf16[4,4,32,64,128]{4,3,2,1,0:T(8,128)(2,1)} %param.6), kind=kLoop, calls=%fused_computation.23 | loop fusion | flops 2097152 | bytes 16777216 | tf_op jit(solution)/shard_map/neg | solution.py:49
  22.3 14.4 %maximum_maximum_fusion = bf16[4,4,32,128,128]{4,3,2,1,0:T(8,128)(2,1)} fusion(bf16[4,4,32,64,64]{4,3,2,1,0:T(8,128)(2,1)S(1)} %get-tuple-element.25, bf16[4,4,32,64,64]{4,3,2,1,0:T(8,128)(2,1)S(1)} %get-tuple-element.24, bf16[4,4,32,64,128]{4,3,2,1,0:T(8,128)(2,1)} %param.6), kind=kLoop, calls=%fused_computation.2 | loop fusion | flops 50331648 | bytes 33554432 | tf_op jit(solution)/shard_map/concatenate | solution.py:50
  36.7 15.4 %reduce-scatter.3.cloned.1.call-done = bf16[4,2,32,256]{3,2,1,0:T(8,128)(2,1)} async-done(((bf16[32,2,32,256]{3,2,1,0:T(8,128)(2,1)}), bf16[4,2,32,256]{3,2,1,0:T(8,128)(2,1)}) %reduce-scatter.3.cloned.1.call-update) | async-done | bytes 131088 | tf_op jit(solution)/shard_map/reduce_scatter | solution.py:96
  53.6 8.0 %fusion.55 = f32[4,128,1,128]{3,2,1,0:T(1,128)S(1)} fusion(bf16[4,128,128,1]{2,3,1,0:T(2,128)(2,1)S(1)} %reshape.391, bf16[4,128,128,128]{3,2,1,0:T(8,128)(2,1)} %bitcast.167), kind=kOutput, calls=%fused_computation.97 | convolution fusion | flops 16777216 | bytes 17170432 | tf_op jit(solution)/shard_map/zmpi,zmio->zmpo/dot_general | solution.py:41
  63.1 12.6 %copy.49 = bf16[32,256,1,4,64]{4,3,1,0,2:T(4,128)(2,1)} copy(bf16[32,256,1,4,64]{1,4,3,2,0:T(8,128)(2,1)} %param.4) | data formatting | bytes 8388608 | tf_op args[0]
  75.7 11.9 %fusion.56 = f32[32768,64]{1,0:T(8,128)} fusion(bf16[32768,64]{1,0:T(8,128)(2,1)} %bitcast.169, bf16[64,64]{1,0:T(8,128)(2,1)S(1)} %copy-done), kind=kOutput, calls=%fused_computation.98 | convolution fusion | flops 268435456 | bytes 12591104 | tf_op jit(solution)/shard_map/dot_general | solution.py:115
  87.6 14.3 %reshape.358 = f32[32,256,256]{2,1,0:T(8,128)} reshape(f32[32768,64]{1,0:T(8,128)} %fusion.56) | data formatting | bytes 16777216 | tf_op jit(solution)/shard_map/reshape | solution.py:118
  101.9 8.9 %copy.51 = f32[32,256,256]{1,2,0:T(8,128)} copy(f32[32,256,256]{2,1,0:T(8,128)} %reshape.358) | data formatting | bytes 16777216 | tf_op jit(solution)/shard_map/reshape | solution.py:118
  112.8 11.9 %fusion.2 = (bf16[32,256,256]{1,2,0:T(8,128)(2,1)S(1)}, bf16[32,256,256]{1,2,0:T(8,128)(2,1)}) fusion(bf16[32,256,1,4,64]{1,4,3,2,0:T(8,128)(2,1)} %param.5, f32[32,256,256]{1,2,0:T(8,128)} %copy.51, f32[32]{0:T(128)S(1)} %compare_select_fusion, bf16[1,32,256]{2,1,0:T(8,128)(2,1)S(1)} %get-tuple-element.31, bf16[1,32,256]{2,1,0:T(8,128)(2,1)S(1)} %get-tuple-element.32, ...), kind=kOutput, calls=%fused_computation.11 | convolution fusion | flops 318832640 | bytes 22052992 | tf_op jit(solution)/shard_map/yrk,xrkq->xyq/dot_general | solution.py:41
  124.8 2.0 copy-done.2
  128.2 6.4 %copy.58 = bf16[32,256,256]{2,1,0:T(8,128)(2,1)} copy(bf16[32,256,256]{1,2,0:T(8,128)(2,1)} %copy-done.2) | data formatting | bytes 8388608 | tf_op jit(solution)/shard_map/convert_element_type | solution.py:124
  136.5 11.1 %reshape.364 = bf16[32768,64]{1,0:T(8,128)(2,1)} reshape(bf16[32,256,256]{2,1,0:T(8,128)(2,1)} %copy.58) | data formatting | bytes 8388608 | tf_op jit(solution)/shard_map/reshape | solution.py:145
  147.7 8.2 %convolution_bitcast_fusion = f32[64,64]{0,1:T(8,128)S(1)} fusion(bf16[32768,64]{1,0:T(8,128)(2,1)} %reshape.364, bf16[32768,64]{1,0:T(8,128)(2,1)} %bitcast.170), kind=kOutput, calls=%fused_computation.38 | convolution fusion | flops 268435456 | bytes 8404992 | tf_op jit(solution)/shard_map/dot_general | solution.py:125
  155.9 19.1 %psum.14 = f32[64,64]{0,1:T(8,128)S(1)} all-reduce(f32[64,64]{0,1:T(8,128)S(1)} %convolution_bitcast_fusion), channel_id=1, replica_groups=mesh['dp'=4,'mp'=8] {'dp'}, use_global_device_ids=true, to_apply=%region_2.3 | all-reduce | flops 4096 | bytes 32768 | tf_op jit(solution)/shard_map/psum | solution.py:133
  175.0 22.6 %psum.15 = f32[64,64]{0,1:T(8,128)S(1)} all-reduce(f32[64,64]{0,1:T(8,128)S(1)} %psum.14), channel_id=1, replica_groups=mesh['dp'=4,'mp'=8] {'mp'}, use_global_device_ids=true, to_apply=%region_3.4 | all-reduce | flops 4096 | bytes 32768 | tf_op jit(solution)/shard_map/psum | solution.py:133
  198.3 11.9 %fusion.58 = f32[32768,64]{1,0:T(8,128)} fusion(bf16[32768,64]{1,0:T(8,128)(2,1)} %reshape.364, bf16[64,64]{1,0:T(8,128)(2,1)S(1)} %copy-done), kind=kOutput, calls=%fused_computation.100 | convolution fusion | flops 268435456 | bytes 12591104 | tf_op jit(solution)/shard_map/dot_general | solution.py:144
  210.1 14.4 %reshape.365 = f32[32,256,256]{2,1,0:T(8,128)} reshape(f32[32768,64]{1,0:T(8,128)} %fusion.58) | data formatting | bytes 16777216 | tf_op jit(solution)/shard_map/reshape | solution.py:147
  224.5 9.0 %copy.60 = f32[32,256,256]{1,2,0:T(8,128)} copy(f32[32,256,256]{2,1,0:T(8,128)} %reshape.365) | data formatting | bytes 16777216 | tf_op jit(solution)/shard_map/reshape | solution.py:147
  235.2 12.2 %fusion.57 = f32[4,128,1,128]{3,2,1,0:T(1,128)S(1)} fusion(bf16[4,128,128,1]{2,3,1,0:T(2,128)(2,1)S(1)} %reshape.393, bf16[4,128,128,128]{3,2,1,0:T(8,128)(2,1)} %bitcast.168), kind=kOutput, calls=%fused_computation.99 | convolution fusion | flops 16777216 | bytes 17170432 | tf_op jit(solution)/shard_map/zmpo,zmio->zmpi/dot_general | solution.py:41
  248.8 11.4 %broadcast_multiply_fusion = f32[4,128,128,128]{3,2,1,0:T(8,128)} fusion(f32[4,128,128]{2,1,0:T(8,128)S(1)} %convert.35, f32[4,128,128]{2,1,0:T(8,128)S(1)} %convert.34), kind=kLoop, calls=%fused_computation.4 | loop fusion | flops 8388608 | bytes 34078720 | tf_op jit(solution)/shard_map/zmpi,zmpo->zmio/dot_general | solution.py:41
  260.2 34.3 %slice_add_fusion = (f32[4,128,64,64]{3,2,1,0:T(8,128)}, f32[4,128,64,64]{3,2,1,0:T(8,128)}) fusion(f32[4,128,128,128]{3,2,1,0:T(8,128)} %broadcast_multiply_fusion), kind=kLoop, calls=%fused_computation.1 | loop fusion | flops 4194304 | bytes 50331648 | tf_op jit(solution)/shard_map/add | solution.py:78
  294.5 17.0 %pad_maximum_fusion = f32[4,128,64,128]{3,2,1,0:T(8,128)} fusion(f32[4,128,64,64]{3,2,1,0:T(8,128)} %get-tuple-element.21, f32[4,128,64,64]{3,2,1,0:T(8,128)} %get-tuple-element.20), kind=kLoop, calls=%fused_computation.3 | loop fusion | flops 4194304 | bytes 33554432 | tf_op jit(solution)/shard_map/concatenate | solution.py:78
  313.2 7.4 %fusion.10 = bf16[32,256,256]{1,2,0:T(8,128)(2,1)} fusion(f32[32,256,256]{1,2,0:T(8,128)} %copy.60, bf16[32,2,32,256]{3,0,1,2:T(8,128)(2,1)S(1)} %fusion.23, bf16[1,32,256]{2,1,0:T(8,128)(2,1)S(1)} %get-tuple-element.31, bf16[1,32,256]{2,1,0:T(8,128)(2,1)S(1)} %get-tuple-element.32), kind=kOutput, calls=%fused_computation.20 | convolution fusion | flops 272646144 | bytes 13664256 | tf_op jit(solution)/shard_map/rky,xrkq->xyq/dot_general | solution.py:41
  (48 shorter events, 16.0 us)
Async XLA Ops:
  7.2 68.6 %copy-start = (bf16[64,64]{1,0:T(8,128)(2,1)S(1)}, bf16[64,64]{1,0:T(8,128)(2,1)}, u32[]{:S(2)}) copy-start(bf16[64,64]{1,0:T(8,128)(2,1)} %param.7) | copy-start | bytes 24580
  7.2 44.9 %reduce-scatter.3.cloned.1.call-start = ((), (), s32[]{:S(2)}) async-start(), calls=%async_computation.2 | async-start | bytes 1179648 | tf_op jit(solution)/shard_map/reduce_scatter | solution.py:96
  13.2 97.9 %all-gather.3.cloned.1.call-start = ((), (), s32[]{:S(2)}) async-start(), calls=%async_computation.3 | async-start | bytes 1179648 | tf_op jit(solution)/shard_map/all_gather | solution.py:105
  62.9 170.6 %reduce-scatter.5.cloned.1.call-start = ((), (), s32[]{:S(2)}) async-start(), calls=%async_computation.4 | async-start | bytes 1179648 | tf_op jit(solution)/shard_map/reduce_scatter | solution.py:96
  124.7 2.0 copy-start.2
  136.5 175.0 %all-gather.5.cloned.1.call-start = ((), (), s32[]{:S(2)}) async-start(), calls=%async_computation.5 | async-start | bytes 1179648 | tf_op jit(solution)/shard_map/all_gather | solution.py:105
  294.5 26.1 %copy-start.1 = (bf16[64,64]{1,0:T(8,128)(2,1)S(1)}, bf16[64,64]{1,0:T(8,128)(2,1)}, u32[]{:S(2)}) copy-start(bf16[64,64]{1,0:T(8,128)(2,1)} %param.7) | copy-start | bytes 24580
Sparse Core Ops, SparseCore 0:
  13.3 38.7 reduce-scatter.2
  63.0 23.4 all-gather.2
  136.6 36.0 reduce-scatter.4
  248.8 20.6 all-gather.4
